TPU v7x, 32 devices: a whole 2x2x4 slice. The times are simulated.
32 devices in a mesh: slab: 2 (over y), bx: 8 (over z, x), by: 2 (over core).
Axes of the slice: x: 2, y: 2, z: 4, core: 2. Of those that a mesh axis runs over, the one named last changes fastest.
Arguments:
- phi: float32 [64, 128, 2048], P('slab', 'bx', 'by'), parts along dimension 0, may hold values from -6 to 6
- first_measurement: float32 [128, 2048], P('slab', 'by'), parts along dimension 0, may hold values from 0.5 to 3.5
- second_measurement: float32 [128, 128], P('slab', 'bx'), parts along dimension 0, may hold values from 0.5 to 3.5
- first_view_mask: int32 [128, 2048], P('slab', 'by'), parts along dimension 0, may hold values 0 or 1
- second_view_mask: int32 [128, 128], P('slab', 'bx'), parts along dimension 0, may hold values 0 or 1
- plane_detector_rows: int32 [32], replicated, may hold values from 0 to 63, as said below
Outputs:
- gradient: float32 [64, 128, 2048], P('slab', 'bx', 'by'), parts along dimension 0
There are 2 independent parts, one for each index of `slab`. A program takes and returns all parts, laid end to end along the dimension named above; an argument that names none is the same for every part. Nothing has to cross between parts.
Inputs may be any that keep to these rules, and one draw needn't show every extreme that they name: `plane_detector_rows`: plane z reads detector row 2 z or 2 z + 1; plane 0 reads row 0 and the last plane reads row 63.
All inputs are finite; a program needn't handle non-finite values. No bound on the sum of `first_view_mask` or of `second_view_mask` on one device may be relied on, other than what follows from the above.
Results may differ from a plain program's by a relative error of at most 0.00002.
Values sent between devices are 32-bit elements; how exact they have to be, the bound alone decides.
A program may use at most 64 MiB of HBM per device.

v0:
```python
import jax
import jax.numpy as jnp
from jax import lax
from jax.sharding import PartitionSpec as P

LAMBDA = 0.5
BETA2 = 1.0


def extended(cells, sides, width):
    for axis, dim in sides:
        count = lax.axis_size(axis)
        ends = count - 1
        head = lax.slice_in_dim(cells, 0, width, axis=dim)
        tail = lax.slice_in_dim(cells, cells.shape[dim] - width, cells.shape[dim], axis=dim)
        cells = jnp.concatenate(
            [
                lax.ppermute(tail, axis, [(i, (i + 1) % count) for i in range(ends)]),
                cells,
                lax.ppermute(head, axis, [((i + 1) % count, i) for i in range(ends)]),
            ],
            axis=dim,
        )
    return cells


def curvature_of(padded):
    core = padded[:-1, :-1, :-1]
    grad_z = padded[1:, :-1, :-1] - core
    grad_x = padded[:-1, 1:, :-1] - core
    grad_y = padded[:-1, :-1, 1:] - core
    magnitude = jnp.sqrt(grad_z * grad_z + grad_x * grad_x + grad_y * grad_y + BETA2)
    flux_z = grad_z / magnitude
    flux_x = grad_x / magnitude
    flux_y = grad_y / magnitude
    div_z = flux_z[1:, 1:, 1:] - flux_z[:-1, 1:, 1:]
    div_x = flux_x[1:, 1:, 1:] - flux_x[1:, :-1, 1:]
    div_y = flux_y[1:, 1:, 1:] - flux_y[1:, 1:, :-1]
    return div_z + div_x + div_y


def per_device(
    phi,
    first_measurement,
    second_measurement,
    first_view_mask,
    second_view_mask,
    plane_detector_rows,
):
    planes, cells_x, cells_y = phi.shape
    total_x = cells_x * lax.axis_size("bx")
    total_y = cells_y * lax.axis_size("by")
    tanh_phi = jnp.tanh(phi)
    heav = 0.5 * (1.0 + tanh_phi)
    slope = 0.5 * (1.0 - tanh_phi * tanh_phi)
    part_a = jnp.sum(heav, axis=1)
    part_b = jnp.sum(heav, axis=2)
    first_measured_rows = jnp.take(first_measurement, plane_detector_rows, axis=0)
    first_mask_rows = jnp.take(first_view_mask, plane_detector_rows, axis=0).astype(jnp.float32)
    second_measured_rows = jnp.take(second_measurement, plane_detector_rows, axis=0)
    second_mask_rows = jnp.take(second_view_mask, plane_detector_rows, axis=0).astype(jnp.float32)
    second_projection = lax.psum(part_b, "by") * (4.0 / total_y)
    second_residual = second_mask_rows * (second_projection - second_measured_rows)
    first_projection = lax.psum(part_a, "bx") * (4.0 / total_x)
    first_residual = first_mask_rows * (first_projection - first_measured_rows)
    padded = extended(phi, (("bx", 1), ("by", 2)), 1)
    padded = jnp.pad(padded, ((1, 1), (0, 0), (0, 0)))
    curv = curvature_of(padded)
    return slope * (first_residual[:, None, :] + second_residual[:, :, None]) - LAMBDA * curv


def solution(mesh):
    in_specs = (
        P("slab", "bx", "by"),
        P("slab", "by"),
        P("slab", "bx"),
        P("slab", "by"),
        P("slab", "bx"),
        P(),
    )
    out_specs = P("slab", "bx", "by")
    return jax.shard_map(
        per_device, mesh=mesh, in_specs=in_specs, out_specs=out_specs, check_vma=False
    )
```

profile of v0, /device:TPU:0, one launch (start us, length us, event | category | flops | bytes accessed | tf_op | source)
XLA Modules:
  0.0 121.4 jit_solution(6646163909018269001)
XLA Ops:
  6.5 0.0 copy-start
  6.5 0.0 copy-start.2
  6.5 0.0 copy-start.4
  6.5 0.0 copy-start.5
  6.5 0.0 copy-start.6
  6.5 0.0 all-reduce.3.cloned.1.call-start
  6.6 1.9 %fusion.10 = (f32[32,1,1024]{2,1,0:T(1,128)S(1)}, f32[32,1,1024]{2,1,0:T(1,128)S(1)}) fusion(f32[32,16,1024]{2,1,0:T(8,128)} %param.6), kind=kLoop, calls=%fused_computation.29 | loop fusion | bytes 524288 | tf_op jit(solution)/shard_map/slice | solution.py:15
  8.5 4.9 %collective-permute-start = (f32[32,1,1024]{2,0,1:T(8,128)S(1)}, f32[32,1,1024]{2,0,1:T(8,128)S(1)}, u32[]{:S(2)}, u32[]{:S(2)}) collective-permute-start(f32[32,1,1024]{2,0,1:T(8,128)S(1)} %copy.15), channel_id=1, source_target_pairs={{0,2},{2,4},{4,6},{6,8},{8,10},{10,12},{12,14},{1,3},{3,5},{5,7},{... | collective-permute-start | bytes 393224 | tf_op jit(solution)/shard_map/ppermute | solution.py:18
  13.5 1.3 %collective-permute-start.1 = (f32[32,1,1024]{2,0,1:T(8,128)S(1)}, f32[32,1,1024]{2,0,1:T(8,128)S(1)}, u32[]{:S(2)}, u32[]{:S(2)}) collective-permute-start(f32[32,1,1024]{2,0,1:T(8,128)S(1)} %copy.16), channel_id=1, source_target_pairs={{2,0},{4,2},{6,4},{8,6},{10,8},{12,10},{14,12},{3,1},{5,3},{7,5},{... | collective-permute-start | bytes 393224 | tf_op jit(solution)/shard_map/ppermute | solution.py:20
  14.8 2.9 %fusion.5 = (f32[32,1024]{1,0:T(8,128)}, f32[32,16]{1,0:T(8,128)S(1)}) fusion(f32[32,16,1024]{2,1,0:T(8,128)} %param.6), kind=kLoop, calls=%fused_computation.19 | loop fusion | flops 2063872 | bytes 2230272 | tf_op jit(solution)/shard_map/reduce_sum | solution.py:56
  17.7 0.0 all-reduce.3.cloned.1.call-update
  17.7 0.7 compare_select_fusion
  18.4 0.7 compare_and_fusion
  19.0 0.0 copy-done
  19.0 0.6 gather_fusion
  19.7 0.0 copy-done.4
  19.7 0.6 gather_fusion.1
  20.3 0.0 copy-done.5
  20.3 0.1 copy.9
  20.4 0.6 gather_fusion.2
  21.0 0.0 copy-done.6
  21.0 0.1 copy.10
  21.1 0.6 gather_fusion.3
  21.6 3.4 %psum.15 = f32[32,16]{1,0:T(8,128)S(1)} all-reduce(f32[32,16]{1,0:T(8,128)S(1)} %get-tuple-element.6), channel_id=1, replica_groups=mesh['slab'=2,'bx'=8,'by'=2] {'by'}, use_global_device_ids=true, to_apply=%region_3.4 | all-reduce | flops 512 | bytes 4096 | tf_op jit(solution)/shard_map/psum | solution.py:62
  25.0 0.1 subtract_multiply_fusion.1
  25.1 0.0 collective-permute-done
  25.1 0.1 copy.13
  25.2 0.0 collective-permute-done.1
  25.2 0.1 copy.14
  25.4 0.0 copy-done.2
  25.4 0.5 pad_maximum_fusion
  25.9 0.0 copy-start.3
  25.9 1.7 %copy-done.3 = f32[32,18,1024]{2,1,0:T(8,128)} copy-done((f32[32,18,1024]{2,1,0:T(8,128)}, f32[32,18,1024]{2,1,0:T(8,128)S(1)}, u32[]{:S(2)}) %copy-start.3) | copy-done | bytes 2359320
  27.6 1.0 fusion.9
  28.6 2.3 %collective-permute-start.2 = (f32[32,18,1]{2,1,0:T(8,128)}, f32[32,18,1]{2,1,0:T(8,128)S(1)}, u32[]{:S(2)}, u32[]{:S(2)}) collective-permute-start(f32[32,18,1]{2,1,0:T(8,128)} %get-tuple-element.12), channel_id=1, source_target_pairs={{0,1},{2,3},{4,5},{6,7},{8,9},{10,11},{12,13},{14,15},{16,17},{18,... | collective-permute-start | bytes 6920 | tf_op jit(solution)/shard_map/ppermute | solution.py:18
  30.8 1.3 %collective-permute-start.3 = (f32[32,18,1]{2,1,0:T(8,128)}, f32[32,18,1]{2,1,0:T(8,128)}, u32[]{:S(2)}, u32[]{:S(2)}) collective-permute-start(f32[32,18,1]{2,1,0:T(8,128)} %get-tuple-element.11), channel_id=1, source_target_pairs={{1,0},{3,2},{5,4},{7,6},{9,8},{11,10},{13,12},{15,14},{17,16},{19,... | collective-permute-start | bytes 6920 | tf_op jit(solution)/shard_map/ppermute | solution.py:20
  32.1 58.6 %all-reduce.3.cloned.1.call-done = f32[32,1024]{1,0:T(8,128)} async-done(((f32[32,1024]{1,0:T(8,128)}), f32[32,1024]{1,0:T(8,128)}) %all-reduce.3.cloned.1.call-update) | async-done | bytes 131088 | tf_op jit(solution)/shard_map/psum | solution.py:64
  90.8 1.0 subtract_multiply_fusion
  91.8 0.0 collective-permute-done.2
  91.8 0.0 collective-permute-done.3
  91.8 4.8 %concatenate.7 = f32[32,18,1026]{2,1,0:T(8,128)} concatenate(f32[32,18,1]{2,1,0:T(8,128)S(1)} %collective-permute-done.2, f32[32,18,1024]{2,1,0:T(8,128)} %copy-done.3, f32[32,18,1]{2,1,0:T(8,128)} %collective-permute-done.3), dimensions={2} | concatenate | bytes 4727808 | tf_op jit(solution)/shard_map/concatenate | solution.py:16
  96.6 0.0 copy-start.1
  96.6 11.4 %fusion.6 = (f32[33,17,1025]{2,1,0:T(8,128)S(1)}, f32[33,17,1025]{2,1,0:T(8,128)S(1)}) fusion(f32[32,18,1026]{2,1,0:T(8,128)} %concatenate.7), kind=kLoop, calls=%fused_computation.20 | loop fusion | flops 6325275 | bytes 6964104 | tf_op jit(solution)/shard_map/div | solution.py:33
  108.1 0.0 copy-done.1
  108.1 1.5 %fusion.7 = (f32[33,17,1025]{2,1,0:T(8,128)S(1)}, f32[33,17,1025]{2,1,0:T(8,128)S(1)}) fusion(f32[33,17,1025]{2,1,0:T(8,128)S(1)} %get-tuple-element.8, f32[32,18,1026]{2,1,0:T(8,128)S(1)} %copy-done.1), kind=kLoop, calls=%fused_computation.21 | loop fusion | flops 2300100 | bytes 9264204 | tf_op jit(solution)/shard_map/div | solution.py:34
  109.6 4.9 %fusion.2 = f32[32,16,1024]{2,1,0:T(8,128)} fusion(f32[33,17,1025]{2,1,0:T(8,128)S(1)} %get-tuple-element.10, f32[33,17,1025]{2,1,0:T(8,128)S(1)} %get-tuple-element.9, f32[33,17,1025]{2,1,0:T(8,128)S(1)} %get-tuple-element.7, f32[32,16,1024]{2,1,0:T(8,128)S(1)} %copy-done.2, f32[32,16]{1,0:T(8,128)S(1)} %subtract_multiply_fusion.1, ...), kind=kLoop, calls=%fused_computation.13 | loop fusion | flops 6291456 | bytes 16910336 | tf_op jit(solution)/shard_map/sub | solution.py:69
  (3 shorter events, 0.1 us)
Async XLA Ops:
  6.5 12.5 %copy-start = (s32[64,1024]{1,0:T(8,128)S(1)}, s32[64,1024]{1,0:T(8,128)}, u32[]{:S(2)}) copy-start(s32[64,1024]{1,0:T(8,128)} %param.9) | copy-start | bytes 786436
  6.5 18.8 %copy-start.2 = (f32[32,16,1024]{2,1,0:T(8,128)S(1)}, f32[32,16,1024]{2,1,0:T(8,128)}, u32[]{:S(2)}) copy-start(f32[32,16,1024]{2,1,0:T(8,128)} %param.6) | copy-start | bytes 6291460
  6.5 13.1 %copy-start.4 = (f32[64,1024]{1,0:T(8,128)S(1)}, f32[64,1024]{1,0:T(8,128)}, u32[]{:S(2)}) copy-start(f32[64,1024]{1,0:T(8,128)} %param.7) | copy-start | bytes 786436
  6.5 13.8 %copy-start.5 = (s32[64,16]{0,1:T(8,128)S(1)}, s32[64,16]{0,1:T(8,128)}, u32[]{:S(2)}) copy-start(s32[64,16]{0,1:T(8,128)} %param.10) | copy-start | bytes 12292
  6.5 14.4 %copy-start.6 = (f32[64,16]{0,1:T(8,128)S(1)}, f32[64,16]{0,1:T(8,128)}, u32[]{:S(2)}) copy-start(f32[64,16]{0,1:T(8,128)} %param.8) | copy-start | bytes 12292
  6.5 84.2 %all-reduce.3.cloned.1.call-start = ((), (), s32[]{:S(2)}) async-start(), calls=%async_computation | async-start | bytes 262144 | tf_op jit(solution)/shard_map/psum | solution.py:64
  8.5 16.5 %collective-permute-start = (f32[32,1,1024]{2,0,1:T(8,128)S(1)}, f32[32,1,1024]{2,0,1:T(8,128)S(1)}, u32[]{:S(2)}, u32[]{:S(2)}) collective-permute-start(f32[32,1,1024]{2,0,1:T(8,128)S(1)} %copy.15), channel_id=1, source_target_pairs={{0,2},{2,4},{4,6},{6,8},{8,10},{10,12},{12,14},{1,3},{3,5},{5,7},{... | collective-permute-start | bytes 393224 | tf_op jit(solution)/shard_map/ppermute | solution.py:18
  13.5 11.7 %collective-permute-start.1 = (f32[32,1,1024]{2,0,1:T(8,128)S(1)}, f32[32,1,1024]{2,0,1:T(8,128)S(1)}, u32[]{:S(2)}, u32[]{:S(2)}) collective-permute-start(f32[32,1,1024]{2,0,1:T(8,128)S(1)} %copy.16), channel_id=1, source_target_pairs={{2,0},{4,2},{6,4},{8,6},{10,8},{12,10},{14,12},{3,1},{5,3},{7,5},{... | collective-permute-start | bytes 393224 | tf_op jit(solution)/shard_map/ppermute | solution.py:20
  25.9 1.7 %copy-start.3 = (f32[32,18,1024]{2,1,0:T(8,128)}, f32[32,18,1024]{2,1,0:T(8,128)S(1)}, u32[]{:S(2)}) copy-start(f32[32,18,1024]{2,1,0:T(8,128)S(1)} %pad_maximum_fusion) | copy-start | bytes 7077892
  28.6 63.2 %collective-permute-start.2 = (f32[32,18,1]{2,1,0:T(8,128)}, f32[32,18,1]{2,1,0:T(8,128)S(1)}, u32[]{:S(2)}, u32[]{:S(2)}) collective-permute-start(f32[32,18,1]{2,1,0:T(8,128)} %get-tuple-element.12), channel_id=1, source_target_pairs={{0,1},{2,3},{4,5},{6,7},{8,9},{10,11},{12,13},{14,15},{16,17},{18,... | collective-permute-start | bytes 6920 | tf_op jit(solution)/shard_map/ppermute | solution.py:18
  30.8 60.9 %collective-permute-start.3 = (f32[32,18,1]{2,1,0:T(8,128)}, f32[32,18,1]{2,1,0:T(8,128)}, u32[]{:S(2)}, u32[]{:S(2)}) collective-permute-start(f32[32,18,1]{2,1,0:T(8,128)} %get-tuple-element.11), channel_id=1, source_target_pairs={{1,0},{3,2},{5,4},{7,6},{9,8},{11,10},{13,12},{15,14},{17,16},{19,... | collective-permute-start | bytes 6920 | tf_op jit(solution)/shard_map/ppermute | solution.py:20
  96.6 11.4 %copy-start.1 = (f32[32,18,1026]{2,1,0:T(8,128)S(1)}, f32[32,18,1026]{2,1,0:T(8,128)}, u32[]{:S(2)}) copy-start(f32[32,18,1026]{2,1,0:T(8,128)} %concatenate.7) | copy-start | bytes 7091716
Sparse Core Ops, SparseCore 0:
  17.8 72.8 all-reduce.2
where the time goes:
time: 122 us; the launch traced here: 121 us
  waiting for transfers between devices  58.7 us (48%)
  other arithmetic  23.7 us (19%)
  between operations  13.6 us (11%)
  local copies, waits for them, and re-layouts  12.3 us (10%)
  starting transfers between devices  9.76 us (8%)
  blocking collectives  3.36 us (3%)
    psum x1, waiting for transfers between devices, per_device(): first_projection = lax.psum(part_a, 'bx') * (4.0 / total_x)  58.6 us
    div x1, other arithmetic, curvature_of(): flux_z = grad_z / magnitude  11.4 us
    ppermute x2, starting transfers between devices, extended(): lax.ppermute(tail, axis, [(i, (i + 1) % count) for i in range(ends)])  7.14 us
    sub x1, other arithmetic, per_device(): slope * (first_residual[:, None, :] + second_residual[:, :, None])  4.89 us
    concatenate x1, local copies, waits for them, and re-layouts, extended(): jnp.concatenate([lax.ppermute(tail, axis, [(i, (i + 1) % count) for i in...  4.83 us
    psum x1, blocking collectives, per_device(): second_projection = lax.psum(part_b, 'by') * (4.0 / total_y)  3.36 us
    reduce_sum x1, other arithmetic, per_device(): part_a = jnp.sum(heav, axis=1)  2.91 us
    ppermute x2, starting transfers between devices, extended(): lax.ppermute(head, axis, [((i + 1) % count, i) for i in range(ends)])  2.58 us
  transfers between devices with their start and end apart: 5, of which 1 were waited for; matrix products, arithmetic and copies ran while one was open for 8% of the time, Pallas kernels for 0%

commit v1 on v0

--- a/solution.py
+++ b/solution.py
@@ -1,10 +1,366 @@
+import functools
+
 import jax
 import jax.numpy as jnp
 from jax import lax
+from jax.experimental import pallas as pl
+from jax.experimental.pallas import tpu as pltpu
 from jax.sharding import PartitionSpec as P
 
 LAMBDA = 0.5
 BETA2 = 1.0
+TILE = 128
+GROUP = 8
+MESH = pl.DeviceIdType.MESH
+
+
+def exchange_kernel(
+    n, phi_hbm, ma_hbm, mb_hbm, va_hbm, vb_hbm, rows_hbm,
+    base_hbm, ra_hbm, rb_hbm,
+    ext, out, esend_recv, sums, rs_recv, pieces, ra_out, bsum, bsum_recv, rb,
+    x_first, x_last, h_next, h_prev, corner, flux_prev,
+    ma, va, mb, vb, rows,
+    in_sem, small_sem, out_sem, fin_sem,
+    rs_send, rs_sem, ag_send, ag_sem, pair_send, pair_sem, halo_send, halo_sem,
+):
+    planes, cells_x, cells_y = phi_hbm.shape
+    groups = planes // GROUP
+    me = lax.axis_index("bx")
+    half = lax.axis_index("by")
+    other = 1 - half
+    total_x = cells_x * n
+    total_y = cells_y * 2
+
+    barrier = pltpu.get_barrier_semaphore()
+    for k in range(1, n):
+        pl.semaphore_signal(barrier, inc=1, device_id={"bx": lax.rem(me + k, n)}, device_id_type=MESH)
+    for k in range(n):
+        pl.semaphore_signal(
+            barrier, inc=1, device_id={"bx": lax.rem(me + k, n), "by": other}, device_id_type=MESH
+        )
+
+    def load(g):
+        return pltpu.make_async_copy(
+            phi_hbm.at[pl.ds(g * GROUP, GROUP)],
+            ext.at[pl.ds(g * GROUP, GROUP), :, pl.ds(TILE, cells_y)],
+            in_sem.at[g],
+        )
+
+    for g in range(groups):
+        load(g).start()
+    lanes_me = pl.ds(pl.multiple_of(me * TILE, TILE), TILE)
+    small = [
+        pltpu.make_async_copy(ma_hbm.at[:, lanes_me], ma, small_sem.at[0]),
+        pltpu.make_async_copy(va_hbm.at[:, lanes_me], va, small_sem.at[1]),
+        pltpu.make_async_copy(mb_hbm, mb, small_sem.at[2]),
+        pltpu.make_async_copy(vb_hbm, vb, small_sem.at[3]),
+        pltpu.make_async_copy(rows_hbm, rows, small_sem.at[4]),
+    ]
+    for copy in small:
+        copy.start()
+
+    for g in range(groups):
+        load(g).wait()
+
+        def first_pass(c, _, g=g):
+            at = pl.ds(g * GROUP, GROUP)
+            cells = ext[at, :, pl.ds(pl.multiple_of(TILE + c * TILE, TILE), TILE)]
+            t = jnp.tanh(cells)
+            sums[c, at, :] = jnp.sum(t, axis=1)
+            cols = pl.ds(pl.multiple_of(c * TILE, TILE), TILE)
+            x_first[at, cols] = cells[:, 0, :]
+            x_last[at, cols] = cells[:, cells_x - 1, :]
+            return _ + t
+
+        bsum[pl.ds(g * GROUP, GROUP)] = lax.fori_loop(
+            0, n, first_pass, jnp.zeros((GROUP, cells_x, TILE), jnp.float32)
+        )
+
+    pl.semaphore_wait(barrier, 2 * n - 1)
+
+    def scatter(k):
+        to = lax.rem(me + k, n)
+        return pltpu.make_async_remote_copy(
+            src_ref=sums.at[to], dst_ref=rs_recv.at[n - k], send_sem=rs_send.at[k],
+            recv_sem=rs_sem.at[n - k], device_id={"bx": to}, device_id_type=MESH,
+        )
+
+    def gather(k):
+        to = lax.rem(me + k, n)
+        return pltpu.make_async_remote_copy(
+            src_ref=pieces.at[me], dst_ref=pieces.at[me], send_sem=ag_send.at[k],
+            recv_sem=ag_sem.at[n - k], device_id={"bx": to}, device_id_type=MESH,
+        )
+
+    def pair(i):
+        edge = pl.ds(pl.multiple_of(TILE + other * (cells_y - TILE), TILE), TILE)
+        src, dst = ((ext.at[pl.ds(0, planes), :, edge], esend_recv), (bsum, bsum_recv))[i]
+        return pltpu.make_async_remote_copy(
+            src_ref=src, dst_ref=dst, send_sem=pair_send.at[i], recv_sem=pair_sem.at[i],
+            device_id={"by": other}, device_id_type=MESH,
+        )
+
+    def to_next():
+        return pltpu.make_async_remote_copy(
+            src_ref=x_last, dst_ref=h_prev, send_sem=halo_send.at[0], recv_sem=halo_sem.at[0],
+            device_id={"bx": lax.rem(me + 1, n)}, device_id_type=MESH,
+        )
+
+    def to_prev():
+        return pltpu.make_async_remote_copy(
+            src_ref=x_first, dst_ref=h_next, send_sem=halo_send.at[1], recv_sem=halo_sem.at[1],
+            device_id={"bx": lax.rem(me + n - 1, n)}, device_id_type=MESH,
+        )
+
+    def corner_prev():
+        return pltpu.make_async_remote_copy(
+            src_ref=x_first.at[:, pl.ds(cells_y - TILE, TILE)], dst_ref=corner,
+            send_sem=halo_send.at[2], recv_sem=halo_sem.at[2],
+            device_id={"bx": lax.rem(me + n - 1, n), "by": other}, device_id_type=MESH,
+        )
+
+    def corner_next():
+        return pltpu.make_async_remote_copy(
+            src_ref=x_last.at[:, pl.ds(0, TILE)], dst_ref=corner,
+            send_sem=halo_send.at[2], recv_sem=halo_sem.at[2],
+            device_id={"bx": lax.rem(me + 1, n), "by": other}, device_id_type=MESH,
+        )
+
+    has_next = me < n - 1
+    has_prev = me > 0
+    for k in range(1, n):
+        scatter(k).start()
+    for i in range(2):
+        pair(i).start()
+
+    @pl.when(has_next)
+    def _():
+        to_next().start()
+
+    @pl.when(has_prev)
+    def _():
+        to_prev().start()
+
+    @pl.when(jnp.logical_and(has_prev, half == 0))
+    def _():
+        corner_prev().start()
+
+    @pl.when(jnp.logical_and(has_next, half == 1))
+    def _():
+        corner_next().start()
+
+    for copy in small:
+        copy.wait()
+    own = lax.broadcasted_iota(jnp.int32, (planes, planes), 0)
+    across = lax.broadcasted_iota(jnp.int32, (planes, planes), 1)
+    offsets = (rows[...] - 2 * across).astype(jnp.float32)
+    odd = jnp.sum(jnp.where(own == across, offsets, 0.0), axis=1, keepdims=True) > 0.5
+
+    def rows_of(ref):
+        low = ref[pl.ds(0, planes, stride=2), :].astype(jnp.float32)
+        high = ref[pl.ds(1, planes, stride=2), :].astype(jnp.float32)
+        return jnp.where(odd, high, low)
+
+    measured_a = rows_of(ma)
+    mask_a = rows_of(va)
+    measured_b = jnp.transpose(rows_of(mb))
+    mask_b = jnp.transpose(rows_of(vb))
+
+    total = sums[me]
+    for k in range(1, n):
+        scatter(n - k).wait_recv()
+        total = total + rs_recv[k]
+    pieces[me] = mask_a * ((2.0 + (2.0 / total_x) * total) - measured_a)
+    for k in range(1, n):
+        gather(k).start()
+
+    pair(0).wait_recv()
+    pair(1).wait_recv()
+    column = lax.broadcasted_iota(jnp.int32, (cells_x, planes), 1)
+
+    def second_view(z, _):
+        pick = column == z
+        both = jnp.sum(bsum[z] + bsum_recv[z], axis=1, keepdims=True)
+        meas = jnp.sum(jnp.where(pick, measured_b, 0.0), axis=1, keepdims=True)
+        mask = jnp.sum(jnp.where(pick, mask_b, 0.0), axis=1, keepdims=True)
+        res = mask * ((2.0 + (2.0 / total_y) * both) - meas)
+        rb[z] = jnp.broadcast_to(res, (cells_x, TILE))
+        return _
+
+    lax.fori_loop(0, planes, second_view, 0)
+    rb_copy = pltpu.make_async_copy(rb, rb_hbm, fin_sem.at[0])
+    rb_copy.start()
+
+    lane3 = lax.broadcasted_iota(jnp.int32, (GROUP, cells_x, TILE), 2)
+    keep3 = lane3 == half * (TILE - 1)
+    for g in range(groups):
+        at = pl.ds(g * GROUP, GROUP)
+        ext[at, :, pl.ds(0, TILE)] = jnp.where(keep3, esend_recv[at], 0.0)
+    ext[planes] = jnp.zeros((cells_x, cells_y + TILE), jnp.float32)
+
+    @pl.when(has_prev)
+    def _():
+        to_next().wait_recv()
+
+    @pl.when(jnp.logical_not(has_prev))
+    def _():
+        h_prev[...] = jnp.zeros_like(h_prev)
+
+    @pl.when(has_next)
+    def _():
+        to_prev().wait_recv()
+
+    @pl.when(jnp.logical_not(has_next))
+    def _():
+        h_next[...] = jnp.zeros_like(h_next)
+
+    has_corner = jnp.logical_or(
+        jnp.logical_and(has_prev, half == 0), jnp.logical_and(has_next, half == 1)
+    )
+
+    @pl.when(has_corner)
+    def _():
+        corner_prev().wait_recv()
+
+    @pl.when(jnp.logical_not(has_corner))
+    def _():
+        corner[...] = jnp.zeros_like(corner)
+
+    lane2 = lax.broadcasted_iota(jnp.int32, (planes, TILE), 1)
+    corners = jnp.where(lane2 == half * (TILE - 1), corner[...], 0.0)
+    width = cells_y + TILE
+    before = jnp.concatenate([corners, h_prev[...]], axis=1)
+    first = jnp.concatenate([jnp.zeros((planes, TILE), jnp.float32), x_first[...]], axis=1)
+    above = pltpu.roll(before, planes - 1, axis=0)
+    level = lax.broadcasted_iota(jnp.int32, (planes, width), 0)
+    gz = jnp.where(level == planes - 1, 0.0, above) - before
+    gx = first - before
+    gy = pltpu.roll(before, width - 1, axis=1) - before
+    flux_prev[...] = LAMBDA * gx * lax.rsqrt(gz * gz + gx * gx + gy * gy + BETA2)
+
+    row = lax.broadcasted_iota(jnp.int32, (cells_x, width), 0)
+
+    def curvature(z, flux_z_before):
+        cells = ext[z]
+        beyond = jnp.concatenate(
+            [jnp.where(lane2[:1] == half * (TILE - 1), corner[pl.ds(z, 1), :], 0.0), h_next[pl.ds(z, 1), :]],
+            axis=1,
+        )
+        right = jnp.where(row == cells_x - 1, beyond, pltpu.roll(cells, cells_x - 1, axis=0))
+        gz = ext[z + 1] - cells
+        gx = right - cells
+        gy = pltpu.roll(cells, width - 1, axis=1) - cells
+        scale = LAMBDA * lax.rsqrt(gz * gz + gx * gx + gy * gy + BETA2)
+        fz = gz * scale
+        fx = gx * scale
+        fy = gy * scale
+        fx_before = jnp.where(row == 0, flux_prev[pl.ds(z, 1), :], pltpu.roll(fx, 1, axis=0))
+        fy_before = pltpu.roll(fy, 1, axis=1)
+        div = (fz - flux_z_before) + (fx - fx_before) + (fy - fy_before)
+        out[z] = div[:, TILE:]
+        return fz
+
+    def store(g):
+        at = pl.ds(g * GROUP, GROUP)
+        return pltpu.make_async_copy(out.at[at], base_hbm.at[at], out_sem.at[g])
+
+    flux_z = LAMBDA * ext[0] * lax.rsqrt(ext[0] * ext[0] + BETA2)
+    for g in range(groups):
+        flux_z = lax.fori_loop(g * GROUP, (g + 1) * GROUP, curvature, flux_z)
+        store(g).start()
+
+    for k in range(1, n):
+        gather(k).wait_recv()
+    for c in range(n):
+        ra_out[:, c * TILE:(c + 1) * TILE] = pieces[c]
+    ra_copy = pltpu.make_async_copy(ra_out, ra_hbm, fin_sem.at[1])
+    ra_copy.start()
+
+    for k in range(1, n):
+        scatter(k).wait_send()
+        gather(k).wait_send()
+    pair(0).wait_send()
+    pair(1).wait_send()
+
+    @pl.when(has_next)
+    def _():
+        to_next().wait_send()
+
+    @pl.when(has_prev)
+    def _():
+        to_prev().wait_send()
+
+    @pl.when(jnp.logical_and(has_prev, half == 0))
+    def _():
+        corner_prev().wait_send()
+
+    @pl.when(jnp.logical_and(has_next, half == 1))
+    def _():
+        corner_next().wait_send()
+
+    for g in range(groups):
+        store(g).wait()
+    rb_copy.wait()
+    ra_copy.wait()
+
+
+def finish_kernel(phi, base, ra, rb, grad):
+    planes, cells_x, cells_y = phi.shape
+    for z in range(planes):
+        for c in range(cells_y // TILE):
+            cols = pl.ds(c * TILE, TILE)
+            t = jnp.tanh(phi[z, :, cols])
+            res = ra[pl.ds(z, 1), cols] + rb[z]
+            grad[z, :, cols] = (0.5 - 0.5 * (t * t)) * res - base[z, :, cols]
+
+
+def per_device_kernels(n, phi, ma, mb, va, vb, rows):
+    planes, cells_x, cells_y = phi.shape
+    f32 = jnp.float32
+    dma = pltpu.SemaphoreType.DMA
+    det = ma.shape[0]
+    groups = planes // GROUP
+    any_spec = pl.BlockSpec(memory_space=pl.ANY)
+    vmem = lambda *shape: pltpu.VMEM(shape, f32)
+    base, ra, rb = pl.pallas_call(
+        functools.partial(exchange_kernel, n),
+        out_shape=(
+            jax.ShapeDtypeStruct(phi.shape, f32),
+            jax.ShapeDtypeStruct((planes, cells_y), f32),
+            jax.ShapeDtypeStruct((planes, cells_x, TILE), f32),
+        ),
+        in_specs=[any_spec] * 6,
+        out_specs=(any_spec,) * 3,
+        scratch_shapes=[
+            vmem(planes + 1, cells_x, cells_y + TILE), vmem(planes, cells_x, cells_y),
+            vmem(planes, cells_x, TILE),
+            vmem(n, planes, TILE), vmem(n, planes, TILE), vmem(n, planes, TILE), vmem(planes, cells_y),
+            vmem(planes, cells_x, TILE), vmem(planes, cells_x, TILE), vmem(planes, cells_x, TILE),
+            vmem(planes, cells_y), vmem(planes, cells_y), vmem(planes, cells_y), vmem(planes, cells_y),
+            vmem(planes, TILE), vmem(planes, cells_y + TILE),
+            vmem(det, TILE), pltpu.VMEM((det, TILE), jnp.int32),
+            vmem(det, cells_x), pltpu.VMEM((det, cells_x), jnp.int32),
+            pltpu.VMEM((1, planes), jnp.int32),
+            dma((groups,)), dma((5,)), dma((groups,)), dma((2,)),
+            dma((n,)), dma((n,)), dma((n,)), dma((n,)), dma((2,)), dma((2,)), dma((3,)), dma((3,)),
+        ],
+        compiler_params=pltpu.CompilerParams(
+            collective_id=0, has_side_effects=True, vmem_limit_bytes=24 << 20
+        ),
+    )(phi, ma, mb, va, vb, rows.reshape(1, planes))
+    block = pl.BlockSpec((GROUP, cells_x, cells_y), lambda i: (i, 0, 0))
+    return pl.pallas_call(
+        finish_kernel,
+        grid=(groups,),
+        out_shape=jax.ShapeDtypeStruct(phi.shape, f32),
+        in_specs=[
+            block, block,
+            pl.BlockSpec((GROUP, cells_y), lambda i: (i, 0)),
+            pl.BlockSpec((GROUP, cells_x, TILE), lambda i: (i, 0, 0)),
+        ],
+        out_specs=block,
+        compiler_params=pltpu.CompilerParams(vmem_limit_bytes=16 << 20),
+    )(phi, base, ra, rb)
 
 
 def extended(cells, sides, width):
@@ -48,6 +404,12 @@
     plane_detector_rows,
 ):
     planes, cells_x, cells_y = phi.shape
+    n = lax.axis_size("bx")
+    if lax.axis_size("by") == 2 and n * TILE == cells_y and planes % GROUP == 0:
+        return per_device_kernels(
+            n, phi, first_measurement, second_measurement, first_view_mask, second_view_mask,
+            plane_detector_rows,
+        )
     total_x = cells_x * lax.axis_size("bx")
     total_y = cells_y * lax.axis_size("by")
     tanh_phi = jnp.tanh(phi)

time: 122 us -> 29.4 us (0.24)
  the two profiles are of different devices: /device:TPU:0 before, /device:TPU:2 now
where the time goes in v1:
time: 29.4 us; the launch traced here: 29.1 us
  Pallas kernels  23.4 us (80%)
  local copies, waits for them, and re-layouts  5.7 us (19%)
    pallas_call x1, Pallas kernels, per_device_kernels(): pl.pallas_call(functools.partial(exchange_kernel, n), out_shape=(jax.Shap...  21.3 us
    unnamed x10, local copies, waits for them, and re-layouts  5.7 us
    pallas_call x1, Pallas kernels, per_device_kernels(): pl.pallas_call(finish_kernel, grid=(groups,), out_shape=jax.ShapeDtypeStr...  2.08 us

profile of v1, /device:TPU:2, one launch (start us, length us, event | category | flops | bytes accessed | tf_op | source)
XLA Modules:
  0.0 29.1 jit_solution(14212760853779950682)
XLA Ops:
  0.0 0.8 %copy.7.mb_hbm = f32[64,16]{1,0:T(8,128)S(1)} copy(f32[64,16]{0,1:T(8,128)} %param.8) | data formatting | bytes 8192 | tf_op args[2]
  0.8 0.8 %copy.8.vb_hbm = s32[64,16]{1,0:T(8,128)S(1)} copy(s32[64,16]{0,1:T(8,128)} %param.10) | data formatting | bytes 8192 | tf_op args[4]
  1.6 0.0 copy-start
  1.6 1.6 %copy-done = f32[32,16,1024]{2,1,0:T(8,128)S(1)} copy-done((f32[32,16,1024]{2,1,0:T(8,128)S(1)}, f32[32,16,1024]{2,1,0:T(8,128)}, u32[]{:S(2)}) %copy-start) | copy-done | bytes 2097176
  3.2 0.0 copy-start.1
  3.2 0.9 %copy-done.1 = f32[64,1024]{1,0:T(8,128)S(1)} copy-done((f32[64,1024]{1,0:T(8,128)S(1)}, f32[64,1024]{1,0:T(8,128)}, u32[]{:S(2)}) %copy-start.1) | copy-done | bytes 262168
  4.1 0.0 copy-start.2
  4.1 0.9 %copy-done.2 = s32[64,1024]{1,0:T(8,128)S(1)} copy-done((s32[64,1024]{1,0:T(8,128)S(1)}, s32[64,1024]{1,0:T(8,128)}, u32[]{:S(2)}) %copy-start.2) | copy-done | bytes 262168
  5.1 0.0 copy-start.3
  5.1 0.7 %copy-done.3 = s32[32]{0:T(128)S(1)} copy-done((s32[32]{0:T(128)S(1)}, s32[32]{0:T(128)}, u32[]{:S(2)}) %copy-start.3) | copy-done | bytes 152
  5.7 21.3 %shard_map.64 = (f32[32,16,1024]{2,1,0:T(8,128)S(1)}, f32[32,1024]{1,0:T(8,128)S(1)}, f32[32,16,128]{2,1,0:T(8,128)S(1)}) custom-call(f32[32,16,1024]{2,1,0:T(8,128)S(1)} %copy-done, f32[64,1024]{1,0:T(8,128)S(1)} %copy-done.1, f32[64,16]{1,0:T(8,128)S(1)} %copy.7.mb_hbm, s32[64,1024]{1,0:T(8,128)S(1)} %copy-done.2, s32[64,16]{1,0:T(8,128)S(1)} %copy.8.vb_hbm, ...), custom_call_target="tpu_custom_call" | custom-call | tf_op jit(solution)/shard_map/pallas_call | solution.py:325
  27.0 2.1 %shard_map.65 = f32[32,16,1024]{2,1,0:T(8,128)} custom-call(f32[32,16,1024]{2,1,0:T(8,128)S(1)} %copy-done, f32[32,16,1024]{2,1,0:T(8,128)S(1)} %get-tuple-element.8.base, f32[32,1024]{1,0:T(8,128)S(1)} %get-tuple-element.9.ra, f32[32,16,128]{2,1,0:T(8,128)S(1)} %get-tuple-element.10.rb), custom_call_target="tpu_custom_call" | custom-call | tf_op jit(solution)/shard_map/pallas_call | solution.py:352
Async XLA Ops:
  1.6 1.6 %copy-start = (f32[32,16,1024]{2,1,0:T(8,128)S(1)}, f32[32,16,1024]{2,1,0:T(8,128)}, u32[]{:S(2)}) copy-start(f32[32,16,1024]{2,1,0:T(8,128)} %phi.1) | copy-start | bytes 6291460
  3.2 0.9 %copy-start.1 = (f32[64,1024]{1,0:T(8,128)S(1)}, f32[64,1024]{1,0:T(8,128)}, u32[]{:S(2)}) copy-start(f32[64,1024]{1,0:T(8,128)} %ma_hbm.1) | copy-start | bytes 786436
  4.1 0.9 %copy-start.2 = (s32[64,1024]{1,0:T(8,128)S(1)}, s32[64,1024]{1,0:T(8,128)}, u32[]{:S(2)}) copy-start(s32[64,1024]{1,0:T(8,128)} %va_hbm.1) | copy-start | bytes 786436
  5.1 0.7 %copy-start.3 = (s32[32]{0:T(128)S(1)}, s32[32]{0:T(128)}, u32[]{:S(2)}) copy-start(s32[32]{0:T(128)} %param.11) | copy-start | bytes 388

commit v2 on v1

--- a/solution.py
+++ b/solution.py
@@ -18,7 +18,7 @@
     n, phi_hbm, ma_hbm, mb_hbm, va_hbm, vb_hbm, rows_hbm,
     base_hbm, ra_hbm, rb_hbm,
     ext, out, esend_recv, sums, rs_recv, pieces, ra_out, bsum, bsum_recv, rb,
-    x_first, x_last, h_next, h_prev, corner, flux_prev,
+    x_first, x_last, h_next, h_prev, corner, flux_prev, flux_row,
     ma, va, mb, vb, rows,
     in_sem, small_sem, out_sem, fin_sem,
     rs_send, rs_sem, ag_send, ag_sem, pair_send, pair_sem, halo_send, halo_sem,
@@ -149,6 +149,41 @@
     def _():
         corner_next().start()
 
+    def store(g):
+        at = pl.ds(g * GROUP, GROUP)
+        return pltpu.make_async_copy(out.at[at], base_hbm.at[at], out_sem.at[g])
+
+    pair(0).wait_recv()
+    lane3 = lax.broadcasted_iota(jnp.int32, (GROUP, cells_x, TILE), 2)
+    keep3 = lane3 == half * (TILE - 1)
+    for g in range(groups):
+        at = pl.ds(g * GROUP, GROUP)
+        ext[at, :, pl.ds(0, TILE)] = jnp.where(keep3, esend_recv[at], 0.0)
+    ext[planes] = jnp.zeros((cells_x, cells_y + TILE), jnp.float32)
+
+    width = cells_y + TILE
+    row = lax.broadcasted_iota(jnp.int32, (cells_x, width), 0)
+
+    def curvature(z, flux_z_before):
+        cells = ext[z]
+        right = pltpu.roll(cells, cells_x - 1, axis=0)
+        gz = ext[z + 1] - cells
+        gx = right - cells
+        gy = pltpu.roll(cells, width - 1, axis=1) - cells
+        scale = LAMBDA * lax.rsqrt(gz * gz + gx * gx + gy * gy + BETA2)
+        fz = gz * scale
+        fx = gx * scale
+        fy = gy * scale
+        fx_before = jnp.where(row == 0, 0.0, pltpu.roll(fx, 1, axis=0))
+        fy_before = pltpu.roll(fy, 1, axis=1)
+        div = (fz - flux_z_before) + (fx - fx_before) + (fy - fy_before)
+        flux_row[pl.ds(z, 1), :] = fx[cells_x - 2:cells_x - 1, :]
+        out[z] = div[:, TILE:]
+        return fz
+
+    flux_z = LAMBDA * ext[0] * lax.rsqrt(ext[0] * ext[0] + BETA2)
+    flux_z = lax.fori_loop(0, planes // 2, curvature, flux_z)
+
     for copy in small:
         copy.wait()
     own = lax.broadcasted_iota(jnp.int32, (planes, planes), 0)
@@ -163,8 +198,11 @@
 
     measured_a = rows_of(ma)
     mask_a = rows_of(va)
-    measured_b = jnp.transpose(rows_of(mb))
-    mask_b = jnp.transpose(rows_of(vb))
+    measured_b = mb[...]
+    mask_b = vb[...].astype(jnp.float32)
+    detectors = mb.shape[1]
+    detector = lax.broadcasted_iota(jnp.int32, (cells_x, detectors), 1).astype(jnp.float32)
+    wanted = rows[...].astype(jnp.float32)
 
     total = sums[me]
     for k in range(1, n):
@@ -174,12 +212,11 @@
     for k in range(1, n):
         gather(k).start()
 
-    pair(0).wait_recv()
+    lax.fori_loop(planes // 2, planes, curvature, flux_z)
     pair(1).wait_recv()
-    column = lax.broadcasted_iota(jnp.int32, (cells_x, planes), 1)
 
     def second_view(z, _):
-        pick = column == z
+        pick = detector == jnp.sum(jnp.where(across[:1] == z, wanted, 0.0), axis=1, keepdims=True)
         both = jnp.sum(bsum[z] + bsum_recv[z], axis=1, keepdims=True)
         meas = jnp.sum(jnp.where(pick, measured_b, 0.0), axis=1, keepdims=True)
         mask = jnp.sum(jnp.where(pick, mask_b, 0.0), axis=1, keepdims=True)
@@ -191,13 +228,6 @@
     rb_copy = pltpu.make_async_copy(rb, rb_hbm, fin_sem.at[0])
     rb_copy.start()
 
-    lane3 = lax.broadcasted_iota(jnp.int32, (GROUP, cells_x, TILE), 2)
-    keep3 = lane3 == half * (TILE - 1)
-    for g in range(groups):
-        at = pl.ds(g * GROUP, GROUP)
-        ext[at, :, pl.ds(0, TILE)] = jnp.where(keep3, esend_recv[at], 0.0)
-    ext[planes] = jnp.zeros((cells_x, cells_y + TILE), jnp.float32)
-
     @pl.when(has_prev)
     def _():
         to_next().wait_recv()
@@ -228,7 +258,6 @@
 
     lane2 = lax.broadcasted_iota(jnp.int32, (planes, TILE), 1)
     corners = jnp.where(lane2 == half * (TILE - 1), corner[...], 0.0)
-    width = cells_y + TILE
     before = jnp.concatenate([corners, h_prev[...]], axis=1)
     first = jnp.concatenate([jnp.zeros((planes, TILE), jnp.float32), x_first[...]], axis=1)
     above = pltpu.roll(before, planes - 1, axis=0)
@@ -238,35 +267,27 @@
     gy = pltpu.roll(before, width - 1, axis=1) - before
     flux_prev[...] = LAMBDA * gx * lax.rsqrt(gz * gz + gx * gx + gy * gy + BETA2)
 
-    row = lax.broadcasted_iota(jnp.int32, (cells_x, width), 0)
-
-    def curvature(z, flux_z_before):
-        cells = ext[z]
-        beyond = jnp.concatenate(
-            [jnp.where(lane2[:1] == half * (TILE - 1), corner[pl.ds(z, 1), :], 0.0), h_next[pl.ds(z, 1), :]],
-            axis=1,
-        )
-        right = jnp.where(row == cells_x - 1, beyond, pltpu.roll(cells, cells_x - 1, axis=0))
-        gz = ext[z + 1] - cells
-        gx = right - cells
-        gy = pltpu.roll(cells, width - 1, axis=1) - cells
-        scale = LAMBDA * lax.rsqrt(gz * gz + gx * gx + gy * gy + BETA2)
-        fz = gz * scale
-        fx = gx * scale
-        fy = gy * scale
-        fx_before = jnp.where(row == 0, flux_prev[pl.ds(z, 1), :], pltpu.roll(fx, 1, axis=0))
-        fy_before = pltpu.roll(fy, 1, axis=1)
-        div = (fz - flux_z_before) + (fx - fx_before) + (fy - fy_before)
-        out[z] = div[:, TILE:]
-        return fz
-
-    def store(g):
-        at = pl.ds(g * GROUP, GROUP)
-        return pltpu.make_async_copy(out.at[at], base_hbm.at[at], out_sem.at[g])
-
-    flux_z = LAMBDA * ext[0] * lax.rsqrt(ext[0] * ext[0] + BETA2)
+    edge = ext[pl.ds(0, planes), :, pl.ds(0, TILE)][:, cells_x - 1, :]
+    last = jnp.concatenate([edge, x_last[...]], axis=1)
+    after = jnp.concatenate([corners, h_next[...]], axis=1)
+    gz = jnp.where(level == planes - 1, 0.0, pltpu.roll(last, planes - 1, axis=0)) - last
+    gx = after - last
+    gy = pltpu.roll(last, width - 1, axis=1) - last
+    scale = LAMBDA * lax.rsqrt(gz * gz + gx * gx + gy * gy + BETA2)
+    fz = gz * scale
+    fy = gy * scale
+    pad = LAMBDA * last * lax.rsqrt(last * last + BETA2)
+    fz_before = jnp.where(level == 0, pad, pltpu.roll(fz, 1, axis=0))
+    div = (fz - fz_before) + (gx * scale - flux_row[...]) + (fy - pltpu.roll(fy, 1, axis=1))
+    flux_row[...] = div
+
+    def complete(z, _):
+        out[z, pl.ds(cells_x - 1, 1), :] = flux_row[pl.ds(z, 1), pl.ds(TILE, cells_y)]
+        out[z, pl.ds(0, 1), :] = out[z, pl.ds(0, 1), :] - flux_prev[pl.ds(z, 1), pl.ds(TILE, cells_y)]
+        return _
+
+    lax.fori_loop(0, planes, complete, 0)
     for g in range(groups):
-        flux_z = lax.fori_loop(g * GROUP, (g + 1) * GROUP, curvature, flux_z)
         store(g).start()
 
     for k in range(1, n):
@@ -329,7 +350,7 @@
             jax.ShapeDtypeStruct((planes, cells_y), f32),
             jax.ShapeDtypeStruct((planes, cells_x, TILE), f32),
         ),
-        in_specs=[any_spec] * 6,
+        in_specs=[pl.BlockSpec(memory_space=pltpu.HBM)] * 6,
         out_specs=(any_spec,) * 3,
         scratch_shapes=[
             vmem(planes + 1, cells_x, cells_y + TILE), vmem(planes, cells_x, cells_y),
@@ -337,9 +358,9 @@
             vmem(n, planes, TILE), vmem(n, planes, TILE), vmem(n, planes, TILE), vmem(planes, cells_y),
             vmem(planes, cells_x, TILE), vmem(planes, cells_x, TILE), vmem(planes, cells_x, TILE),
             vmem(planes, cells_y), vmem(planes, cells_y), vmem(planes, cells_y), vmem(planes, cells_y),
-            vmem(planes, TILE), vmem(planes, cells_y + TILE),
+            vmem(planes, TILE), vmem(planes, cells_y + TILE), vmem(planes, cells_y + TILE),
             vmem(det, TILE), pltpu.VMEM((det, TILE), jnp.int32),
-            vmem(det, cells_x), pltpu.VMEM((det, cells_x), jnp.int32),
+            vmem(cells_x, det), pltpu.VMEM((cells_x, det), jnp.int32),
             pltpu.VMEM((1, planes), jnp.int32),
             dma((groups,)), dma((5,)), dma((groups,)), dma((2,)),
             dma((n,)), dma((n,)), dma((n,)), dma((n,)), dma((2,)), dma((2,)), dma((3,)), dma((3,)),
@@ -347,7 +368,7 @@
         compiler_params=pltpu.CompilerParams(
             collective_id=0, has_side_effects=True, vmem_limit_bytes=24 << 20
         ),
-    )(phi, ma, mb, va, vb, rows.reshape(1, planes))
+    )(*[pltpu.with_memory_space_constraint(x, pltpu.HBM) for x in (phi, ma, mb.T, va, vb.T, rows.reshape(1, planes))])
     block = pl.BlockSpec((GROUP, cells_x, cells_y), lambda i: (i, 0, 0))
     return pl.pallas_call(
         finish_kernel,

time: 29.4 us -> 21.8 us (0.74)
  the two profiles are of different devices: /device:TPU:2 before, /device:TPU:0 now
where the time goes in v2:
time: 21.8 us; the launch traced here: 21.6 us
  Pallas kernels  21.6 us (99%)
    pallas_call x1, Pallas kernels, per_device_kernels(): pl.pallas_call(functools.partial(exchange_kernel, n), out_shape=(jax.Shap...  19.5 us
    pallas_call x1, Pallas kernels, per_device_kernels(): pl.pallas_call(finish_kernel, grid=(groups,), out_shape=jax.ShapeDtypeStr...  2.06 us

profile of v2, /device:TPU:0, one launch (start us, length us, event | category | flops | bytes accessed | tf_op | source)
XLA Modules:
  0.0 21.6 jit_solution(6453850540082282087)
XLA Ops:
  0.0 0.0 copy-start
  0.0 19.5 %shard_map.64 = (f32[32,16,1024]{2,1,0:T(8,128)S(1)}, f32[32,1024]{1,0:T(8,128)S(1)}, f32[32,16,128]{2,1,0:T(8,128)S(1)}) custom-call(f32[32,16,1024]{2,1,0:T(8,128)} %phi.1, f32[64,1024]{1,0:T(8,128)} %ma_hbm.1, f32[16,64]{1,0:T(8,128)} %bitcast.3, s32[64,1024]{1,0:T(8,128)} %va_hbm.1, s32[16,64]{1,0:T(8,128)} %bitcast.4, s32[1,32]{1,0:T(1,128)} %bitcast.5), custom_call_target="tpu_custom_call" | custom-call | tf_op jit(solution)/shard_map/pallas_call | solution.py:346
  19.5 0.0 copy-done
  19.6 2.1 %shard_map.65 = f32[32,16,1024]{2,1,0:T(8,128)} custom-call(f32[32,16,1024]{2,1,0:T(8,128)S(1)} %copy-done, f32[32,16,1024]{2,1,0:T(8,128)S(1)} %get-tuple-element.8.base, f32[32,1024]{1,0:T(8,128)S(1)} %get-tuple-element.9.ra, f32[32,16,128]{2,1,0:T(8,128)S(1)} %get-tuple-element.10.rb), custom_call_target="tpu_custom_call" | custom-call | tf_op jit(solution)/shard_map/pallas_call | solution.py:373
Async XLA Ops:
  0.0 19.5 %copy-start = (f32[32,16,1024]{2,1,0:T(8,128)S(1)}, f32[32,16,1024]{2,1,0:T(8,128)}, u32[]{:S(2)}) copy-start(f32[32,16,1024]{2,1,0:T(8,128)} %phi.1) | copy-start | bytes 6291460
